TPU v7x, 512 devices: a whole 4x4x16 slice. The times are simulated.
512 devices in a mesh: wide: 64 (over x, z), narrow: 8 (over y, core).
Axes of the slice: x: 4, y: 4, z: 16, core: 2. Of those that a mesh axis runs over, the one named last changes fastest.
Arguments:
- amplitudes: bfloat16 [2048, 8192], P(('wide', 'narrow')), may hold values from -6 to 6
- amp_mask: int32 [32, 128], replicated, may hold values from 0 to 1, as said below
- integrals: bfloat16 [2048, 32768], P('narrow', 'wide'), may hold values from -0.59765625 to 0.59765625
- int_mask: int32 [32, 512], replicated, may hold values from 0 to 1, as said below
- owner: int32 [512], replicated, may hold values from 0 to 511, each once
- occ_energy: float32 [8192], P('narrow'), may hold values from -3 to -0.5
- vir_energy: float32 [32768], replicated, may hold values from 1 to 8
Outputs:
- update: bfloat16 [8192, 32768], P('narrow', 'wide')
Inputs may be any that keep to these rules, and one draw needn't show every extreme that they name: `amp_mask`: 1 marks a pair of tiles within the screening distance, 0 one outside it. `int_mask`: 1 marks a pair of tiles within the screening distance, 0 one outside it. A permutation of the 512 tiles; columns 64 * s to 64 * s + 63 of integrals and update belong to tile owner[s].
All inputs are finite; a program needn't handle non-finite values.
Results may differ from a plain program's by a relative error of at most 0.001.
Values may be sent and summed in bfloat16 or wider, within the bound.
No kernel may reach another device: no remote copies, remote signals or barrier semaphores. Data moves between devices by JAX's collectives and lax.ppermute only.
A program may use at most 64 MiB of HBM per device.

v0:
```python
import jax
import jax.numpy as jnp
from jax import lax
from jax.sharding import PartitionSpec as P

TILE = 64


def contract_rows(summed, rows_in, int_part):
    return summed + lax.dot_general(
        rows_in, int_part, (((0,), (0,)), ((), ())), preferred_element_type=jnp.float32
    )


def contract_all(amp_full, int_full, starting):
    k_total = amp_full.shape[0]
    block_rows = min(512, k_total)
    summed = starting
    for first_row in range(0, k_total, block_rows):
        summed = contract_rows(
            summed,
            amp_full[first_row : first_row + block_rows],
            int_full[first_row : first_row + block_rows],
        )
    return summed


def shards(amplitudes, amp_mask, integrals, int_mask, owner, occ_energy, vir_energy):
    tile_width = TILE
    wide_count = lax.axis_size("wide")
    narrow_count = lax.axis_size("narrow")
    wide_index = lax.axis_index("wide")
    narrow_index = lax.axis_index("narrow")
    src_rows = amplitudes.shape[0]
    occ_all = amplitudes.shape[1]
    occ_here = occ_energy.shape[0]
    vir_here = integrals.shape[1]
    k_total = src_rows * wide_count * narrow_count
    first_src = (wide_index * narrow_count + narrow_index) * src_rows
    src_tiles = (first_src + jnp.arange(src_rows, dtype=jnp.int32)) // tile_width
    src_mask = jnp.take(amp_mask, src_tiles, axis=0)
    src_wide = jnp.broadcast_to(
        src_mask[:, :, None], (src_rows, occ_all // tile_width, tile_width)
    ).reshape(src_rows, occ_all)
    masked = jnp.where(src_wide == 1, amplitudes, jnp.zeros((), amplitudes.dtype))
    vir_tiles_here = vir_here // tile_width
    slot_ids = wide_index * vir_tiles_here + jnp.arange(vir_tiles_here, dtype=jnp.int32)
    tile_ids = jnp.take(owner, slot_ids)
    vir_mask = jnp.take(int_mask, tile_ids, axis=1)
    int_rows = integrals.shape[0]
    row_tiles = int_rows // tile_width
    local_mask = lax.dynamic_slice_in_dim(vir_mask, narrow_index * row_tiles, row_tiles, 0)
    local_wide = jnp.broadcast_to(
        local_mask[:, None, :, None], (row_tiles, tile_width, vir_tiles_here, tile_width)
    ).reshape(int_rows, vir_here)
    int_masked = jnp.where(local_wide == 1, integrals, jnp.zeros((), integrals.dtype))
    int_full = lax.all_gather(int_masked, "narrow", axis=0, tiled=True)
    starting = jnp.zeros((occ_here, vir_here), jnp.float32)
    wide_rows = lax.all_gather(masked, "wide", axis=0, tiled=True)
    blocked = lax.all_to_all(wide_rows, "narrow", split_axis=1, concat_axis=0, tiled=True)
    ordered = (
        blocked.reshape(narrow_count, wide_count, src_rows, occ_here)
        .transpose(1, 0, 2, 3)
        .reshape(k_total, occ_here)
    )
    ladder = contract_all(ordered, int_full, starting)
    vir_energy_here = jnp.take(vir_energy.reshape(-1, tile_width), tile_ids, axis=0).reshape(
        vir_here
    )
    denominator = vir_energy_here[None, :] - occ_energy[:, None]
    return (ladder / denominator).astype(jnp.bfloat16)


def solution(mesh):
    return jax.shard_map(
        shards,
        mesh=mesh,
        in_specs=(
            P(("wide", "narrow"), None),
            P(),
            P("narrow", "wide"),
            P(),
            P(),
            P("narrow"),
            P(),
        ),
        out_specs=P("narrow", "wide"),
        check_vma=False,
    )
```

profile of v0, /device:TPU:1, one launch (start us, length us, event | category | flops | bytes accessed | tf_op | source)
XLA Modules:
  0.0 269.0 jit_solution(17122527610451207436)
XLA Ops:
  7.4 0.7 copy-done
  8.1 0.6 gather_fusion
  9.0 1.5 select_bitcast_fusion
  10.6 1.0 copy.21
  11.6 1.3 gather_fusion.1
  13.5 139.6 %all-gather.6.cloned.1.call-done = bf16[64,4,8192]{2,1,0:T(4,128)(2,1)} async-done(((bf16[1,4,8192]{2,1,0:T(4,128)(2,1)}), bf16[64,4,8192]{2,1,0:T(4,128)(2,1)}) %all-gather.6.cloned.1.call-update) | async-done | bytes 4194320 | tf_op jit(solution)/shard_map/all_gather | solution.py:59
  153.1 7.8 %all_to_all.12 = bf16[256,8,1024]{2,1,0:T(8,128)(2,1)} reshape(bf16[64,4,8192]{2,1,0:T(4,128)(2,1)} %all-gather.6.cloned.1.call-done) | data formatting | bytes 8388608 | tf_op jit(solution)/shard_map/all_to_all | solution.py:60
  160.9 6.5 %copy.18 = bf16[256,8,1024]{2,0,1:T(8,128)(2,1)} copy(bf16[256,8,1024]{2,1,0:T(8,128)(2,1)} %all_to_all.12) | data formatting | bytes 8388608 | tf_op jit(solution)/shard_map/all_to_all | solution.py:60
  167.3 14.7 %all-to-all-start = ((bf16[256,8,1024]{2,0,1:T(8,128)(2,1)}), bf16[256,8,1024]{2,0,1:T(8,128)(2,1)}, u32[]{:S(2)}, u32[]{:S(2)}) async-start(bf16[256,8,1024]{2,0,1:T(8,128)(2,1)} %copy.18), calls=%async_computation | async-start | bytes 8388608 | tf_op jit(solution)/shard_map/all_to_all | solution.py:60
  182.9 0.7 broadcast_select_fusion
  183.7 0.6 gather_fusion.3
  184.5 54.8 %all-to-all-done = bf16[256,8,1024]{2,0,1:T(8,128)(2,1)} async-done(((bf16[256,8,1024]{2,0,1:T(8,128)(2,1)}), bf16[256,8,1024]{2,0,1:T(8,128)(2,1)}, u32[]{:S(2)}, u32[]{:S(2)}) %all-to-all-start) | async-done | bytes 4194336 | tf_op jit(solution)/shard_map/all_to_all | solution.py:60
  239.3 4.5 %copy.19 = bf16[256,8,1024]{2,1,0:T(8,128)(2,1)S(1)} copy(bf16[256,8,1024]{2,0,1:T(8,128)(2,1)} %all-to-all-done) | data formatting | bytes 8388608 | tf_op jit(solution)/shard_map/all_to_all | solution.py:60
  243.8 1.8 fusion.11
  245.6 0.9 copy.25
  246.5 1.1 slice.46
  247.6 0.9 copy.24
  248.8 2.1 copy.23
  251.2 3.1 %copy.20 = bf16[16,8,4,1024]{3,2,1,0:T(4,128)(2,1)} copy(bf16[16,8,4,1024]{3,1,2,0:T(8,128)(2,1)} %get-tuple-element.8) | data formatting | bytes 2097152 | tf_op jit(solution)/shard_map/slice | solution.py:22
  254.3 1.3 slice.37
  255.7 1.9 fusion.1
  257.6 0.8 fusion.3
  258.4 0.7 fusion.5
  259.6 1.9 divide_convert_fusion
  (38 shorter events, 3.1 us)
Async XLA Ops:
  7.4 0.7 copy-start
  7.4 145.7 %all-gather.6.cloned.1.call-start = ((), (), s32[]{:S(2)}) async-start(), calls=%async_computation.2 | async-start | bytes 4259840 | tf_op jit(solution)/shard_map/all_gather | solution.py:59
  167.3 15.5 %copy-start.3 = (bf16[256,512]{1,0:T(8,128)(2,1)S(1)}, bf16[256,512]{1,0:T(8,128)(2,1)}, u32[]{:S(2)}) copy-start(bf16[256,512]{1,0:T(8,128)(2,1)} %param.9) | copy-start | bytes 786436
  167.3 16.3 %copy-start.4 = (f32[32768]{0:T(1024)S(1)}, f32[32768]{0:T(1024)}, u32[]{:S(2)}) copy-start(f32[32768]{0:T(1024)} %param.13) | copy-start | bytes 393220
  167.3 72.0 %all-to-all-start = ((bf16[256,8,1024]{2,0,1:T(8,128)(2,1)}), bf16[256,8,1024]{2,0,1:T(8,128)(2,1)}, u32[]{:S(2)}, u32[]{:S(2)}) async-start(bf16[256,8,1024]{2,0,1:T(8,128)(2,1)} %copy.18), calls=%async_computation | async-start | bytes 8388608 | tf_op jit(solution)/shard_map/all_to_all | solution.py:60
  182.1 73.6 %all-gather.4.cloned.1.call-start = ((), (), s32[]{:S(2)}) async-start(), calls=%async_computation.1 | async-start | bytes 2359296 | tf_op jit(solution)/shard_map/all_gather | solution.py:57
  255.7 1.9 copy-start.1
  258.4 1.2 copy-start.2
  258.4 1.2 copy-start.5
Sparse Core Ops, SparseCore 0:
  11.1 141.9 all-gather.5
Sparse Core Ops, SparseCore 1:
  184.7 34.4 all-gather.3
where the time goes:
time: 270 us; the launch traced here: 269 us
  waiting for transfers between devices  194 us (72%)
  local copies, waits for them, and re-layouts  36.7 us (14%)
  between operations  15 us (6%)
  starting transfers between devices  14.7 us (5%)
  matrix products  5.37 us (2%)
    all_gather x1, waiting for transfers between devices, shards(): wide_rows = lax.all_gather(masked, 'wide', axis=0, tiled=True)  140 us
    all_to_all x1, waiting for transfers between devices, shards(): lax.all_to_all(wide_rows, 'narrow', split_axis=1, concat_axis=0, tiled=True)  54.8 us
    all_to_all x3, local copies, waits for them, and re-layouts, shards(): lax.all_to_all(wide_rows, 'narrow', split_axis=1, concat_axis=0, tiled=True)  18.7 us
    all_to_all x1, starting transfers between devices, shards(): lax.all_to_all(wide_rows, 'narrow', split_axis=1, concat_axis=0, tiled=True)  14.7 us
    slice x9, local copies, waits for them, and re-layouts, contract_all(): amp_full[first_row:first_row + block_rows]  11.8 us
  transfers between devices with their start and end apart: 3, of which 2 were waited for; matrix products, arithmetic and copies ran while one was open for 8% of the time, Pallas kernels for 0%

commit v1 on v0

--- a/solution.py
+++ b/solution.py
@@ -56,7 +56,9 @@
     int_masked = jnp.where(local_wide == 1, integrals, jnp.zeros((), integrals.dtype))
     int_full = lax.all_gather(int_masked, "narrow", axis=0, tiled=True)
     starting = jnp.zeros((occ_here, vir_here), jnp.float32)
-    wide_rows = lax.all_gather(masked, "wide", axis=0, tiled=True)
+    wide_rows = jnp.concatenate(
+        lax.all_to_all(jnp.stack([masked] * lax.axis_size("wide")), "wide", 0, 0), axis=0
+    )
     blocked = lax.all_to_all(wide_rows, "narrow", split_axis=1, concat_axis=0, tiled=True)
     ordered = (
         blocked.reshape(narrow_count, wide_count, src_rows, occ_here)

time: 270 us -> 331 us (1.23)
  waiting for transfers between devices: 194 us -> 237 us
  starting transfers between devices: 14.7 us -> 29.4 us
  local copies, waits for them, and re-layouts: 36.7 us -> 42.4 us
    all_to_all x0 -> x1, waiting for transfers between devices: none -> 182 us  [shards(): lax.all_to_all(jnp.stack([masked] * lax.axis_size('wide')), 'wide', 0, 0)]
    all_gather x1 -> x0, waiting for transfers between devices: 140 us -> none  [shards(): wide_rows = lax.all_gather(masked, 'wide', axis=0, tiled=True)]
    all_to_all x0 -> x1, starting transfers between devices: none -> 19.5 us  [shards(): lax.all_to_all(jnp.stack([masked] * lax.axis_size('wide')), 'wide', 0, 0)]
    all_to_all x1, starting transfers between devices: 14.7 us -> 9.92 us  [shards(): lax.all_to_all(wide_rows, 'narrow', split_axis=1, concat_axis=0, tiled=True)]
    another operation x0 -> x1, local copies, waits for them, and re-layouts: none -> 3.99 us  [shards(): jnp.stack([masked] * lax.axis_size('wide'))]
  transfers between devices with their start and end apart: 3 -> 3, of which waited for: 2 -> 2; matrix products, arithmetic and copies ran while one was open for 8% -> 7% of each run, Pallas kernels for 0% -> 0%
where the time goes in v1:
time: 331 us; the launch traced here: 330 us
  waiting for transfers between devices  237 us (72%)
  local copies, waits for them, and re-layouts  42.4 us (13%)
  starting transfers between devices  29.4 us (9%)
  between operations  13.6 us (4%)
  matrix products  5.37 us (2%)
    all_to_all x1, waiting for transfers between devices, shards(): lax.all_to_all(jnp.stack([masked] * lax.axis_size('wide')), 'wide', 0, 0)  182 us
    all_to_all x1, waiting for transfers between devices, shards(): lax.all_to_all(wide_rows, 'narrow', split_axis=1, concat_axis=0, tiled=True)  54.8 us
    all_to_all x1, starting transfers between devices, shards(): lax.all_to_all(jnp.stack([masked] * lax.axis_size('wide')), 'wide', 0, 0)  19.5 us
    all_to_all x3, local copies, waits for them, and re-layouts, shards(): lax.all_to_all(wide_rows, 'narrow', split_axis=1, concat_axis=0, tiled=True)  18.8 us
    slice x9, local copies, waits for them, and re-layouts, contract_all(): amp_full[first_row:first_row + block_rows]  15 us
    all_to_all x1, starting transfers between devices, shards(): lax.all_to_all(wide_rows, 'narrow', split_axis=1, concat_axis=0, tiled=True)  9.92 us
  transfers between devices with their start and end apart: 3, of which 2 were waited for; matrix products, arithmetic and copies ran while one was open for 7% of the time, Pallas kernels for 0%

profile of v1, /device:TPU:1, one launch (start us, length us, event | category | flops | bytes accessed | tf_op | source)
XLA Modules:
  0.0 329.7 jit_solution(7224053824859371581)
XLA Ops:
  6.6 0.7 copy-done
  7.3 0.6 gather_fusion
  8.2 0.9 broadcast_select_fusion.1
  9.1 4.0 %stack.2 = bf16[64,4,8192]{2,1,0:T(4,128)(2,1)} broadcast(bf16[4,8192]{1,0:T(4,128)(2,1)S(1)} %broadcast_select_fusion.1), dimensions={1,2} | broadcast | bytes 4259840 | tf_op jit(solution)/shard_map/stack | solution.py:60
  13.1 19.5 %all-to-all-start = ((bf16[64,4,8192]{2,1,0:T(4,128)(2,1)}), bf16[64,4,8192]{2,1,0:T(4,128)(2,1)}, u32[]{:S(2)}, u32[]{:S(2)}) async-start(bf16[64,4,8192]{2,1,0:T(4,128)(2,1)} %stack.2), calls=%async_computation | async-start | bytes 8388608 | tf_op jit(solution)/shard_map/all_to_all | solution.py:60
  32.8 0.6 gather_fusion.1
  34.0 182.1 %all-to-all-done = bf16[64,4,8192]{2,1,0:T(4,128)(2,1)} async-done(((bf16[64,4,8192]{2,1,0:T(4,128)(2,1)}), bf16[64,4,8192]{2,1,0:T(4,128)(2,1)}, u32[]{:S(2)}, u32[]{:S(2)}) %all-to-all-start) | async-done | bytes 4194336 | tf_op jit(solution)/shard_map/all_to_all | solution.py:60
  216.1 7.8 %all_to_all.16 = bf16[256,8,1024]{2,1,0:T(8,128)(2,1)} reshape(bf16[64,4,8192]{2,1,0:T(4,128)(2,1)} %all-to-all-done) | data formatting | bytes 8388608 | tf_op jit(solution)/shard_map/all_to_all | solution.py:62
  223.9 6.5 %copy.25 = bf16[256,8,1024]{2,0,1:T(8,128)(2,1)} copy(bf16[256,8,1024]{2,1,0:T(8,128)(2,1)} %all_to_all.16) | data formatting | bytes 8388608 | tf_op jit(solution)/shard_map/all_to_all | solution.py:62
  230.3 9.9 %all-to-all-start.1 = ((bf16[256,8,1024]{2,0,1:T(8,128)(2,1)}), bf16[256,8,1024]{2,0,1:T(8,128)(2,1)}, u32[]{:S(2)}, u32[]{:S(2)}) async-start(bf16[256,8,1024]{2,0,1:T(8,128)(2,1)} %copy.25), calls=%async_computation.1 | async-start | bytes 8388608 | tf_op jit(solution)/shard_map/all_to_all | solution.py:62
  241.0 0.7 broadcast_select_fusion
  242.6 54.8 %all-to-all-done.1 = bf16[256,8,1024]{2,0,1:T(8,128)(2,1)} async-done(((bf16[256,8,1024]{2,0,1:T(8,128)(2,1)}), bf16[256,8,1024]{2,0,1:T(8,128)(2,1)}, u32[]{:S(2)}, u32[]{:S(2)}) %all-to-all-start.1) | async-done | bytes 4194336 | tf_op jit(solution)/shard_map/all_to_all | solution.py:62
  297.5 4.5 %copy.26 = bf16[256,8,1024]{2,1,0:T(8,128)(2,1)S(1)} copy(bf16[256,8,1024]{2,0,1:T(8,128)(2,1)} %all-to-all-done.1) | data formatting | bytes 8388608 | tf_op jit(solution)/shard_map/all_to_all | solution.py:62
  302.0 1.8 fusion.11
  303.7 0.9 copy.31
  304.9 2.1 copy.27
  307.3 3.1 copy.30
  310.4 1.3 slice.40
  311.7 3.1 copy.32
  314.8 2.1 slice.46
  317.0 1.9 fusion.1
  318.9 0.7 fusion.5
  319.7 0.7 fusion.3
  320.9 1.9 divide_convert_fusion
  (42 shorter events, 3.8 us)
Async XLA Ops:
  6.5 0.7 copy-start
  13.1 19.5 %copy-start.6 = (s32[32,512]{1,0:T(8,128)S(1)}, s32[32,512]{1,0:T(8,128)}, u32[]{:S(2)}) copy-start(s32[32,512]{1,0:T(8,128)} %param.10) | copy-start | bytes 196612
  13.1 19.7 %copy-start.1 = (s32[512]{0:T(512)S(1)}, s32[512]{0:T(512)}, u32[]{:S(2)}) copy-start(s32[512]{0:T(512)} %param.11) | copy-start | bytes 6148
  13.1 203.0 %all-to-all-start = ((bf16[64,4,8192]{2,1,0:T(4,128)(2,1)}), bf16[64,4,8192]{2,1,0:T(4,128)(2,1)}, u32[]{:S(2)}, u32[]{:S(2)}) async-start(bf16[64,4,8192]{2,1,0:T(4,128)(2,1)} %stack.2), calls=%async_computation | async-start | bytes 8388608 | tf_op jit(solution)/shard_map/all_to_all | solution.py:60
  230.3 10.7 %copy-start.4 = (bf16[256,512]{1,0:T(8,128)(2,1)S(1)}, bf16[256,512]{1,0:T(8,128)(2,1)}, u32[]{:S(2)}) copy-start(bf16[256,512]{1,0:T(8,128)(2,1)} %param.9) | copy-start | bytes 786436
  230.3 11.5 %copy-start.5 = (f32[32768]{0:T(1024)S(1)}, f32[32768]{0:T(1024)}, u32[]{:S(2)}) copy-start(f32[32768]{0:T(1024)} %param.13) | copy-start | bytes 393220
  230.3 67.1 %all-to-all-start.1 = ((bf16[256,8,1024]{2,0,1:T(8,128)(2,1)}), bf16[256,8,1024]{2,0,1:T(8,128)(2,1)}, u32[]{:S(2)}, u32[]{:S(2)}) async-start(bf16[256,8,1024]{2,0,1:T(8,128)(2,1)} %copy.25), calls=%async_computation.1 | async-start | bytes 8388608 | tf_op jit(solution)/shard_map/all_to_all | solution.py:62
  240.3 76.7 %all-gather.2.cloned.1.call-start = ((), (), s32[]{:S(2)}) async-start(), calls=%async_computation.2 | async-start | bytes 2359296 | tf_op jit(solution)/shard_map/all_gather | solution.py:57
  317.0 1.9 copy-start.2
  319.7 1.2 copy-start.3
  319.7 1.2 copy-start.7
Sparse Core Ops, SparseCore 0:
  243.2 33.0 all-gather.1
